TPU v7x, 256 devices: a whole 4x4x8 slice. The times are simulated.
256 devices in a mesh: ctx: 32 (over z, x), exp: 8 (over y, core).
Axes of the slice: x: 4, y: 4, z: 8, core: 2. Of those that a mesh axis runs over, the one named last changes fastest.
Arguments:
- grad_out: bfloat16 [32768, 2880], P(('ctx', 'exp')), may hold values from -6 to 6
- top_logits: float32 [32768, 4], P(('ctx', 'exp')), may hold values from -8 to 308
- expert_ids: int32 [32768, 4], P(('ctx', 'exp')), may hold values from 0 to 7, all different within a row; in each aligned block of 128 rows (0 to 127, 128 to 255, ...) at most 96 rows name the same one
- saved_hidden: bfloat16 [32, 8, 768, 1536], P('ctx', 'exp'), may hold values from -0.29882812 to 0.29882812
- w_down: bfloat16 [8, 1536, 2880], P('exp', 'ctx'), may hold values from -0.15625 to 0.15625
Outputs:
- logit_grad: float32 [32768, 4], P(('ctx', 'exp'))
- hidden_grad: bfloat16 [32, 8, 768, 1536], P('ctx', 'exp')
- down_grad: float32 [8, 1536, 2880], P('exp', 'ctx')
Inputs may be any that keep to these rules, and one draw needn't show every extreme that they name: `expert_ids`: each row names 4 different experts; among the rows of one device no expert is named by more than 96 rows, a bound that some blocks reach.
All inputs are finite; a program needn't handle non-finite values.
Results may differ from a plain program's by a relative error of at most 0.0048.
Values may be sent and summed in bfloat16 or wider, within the bound.
A program may use at most 128 MiB of HBM per device.

v0:
```python
import jax
import jax.numpy as jnp
from jax import lax
from jax.sharding import PartitionSpec as P


def routing_tables(expert_ids, count_experts, capacity):
    columns = jnp.arange(count_experts, dtype=jnp.int32)
    matches = expert_ids[:, :, None] == columns[None, None, :]
    per_token = jnp.sum(matches.astype(jnp.int32), axis=1)
    rank_table = jnp.cumsum(per_token, axis=0) - per_token
    slot_iota = jnp.arange(capacity, dtype=jnp.int32)
    select = (per_token.T[:, None, :] == 1) & (rank_table.T[:, None, :] == slot_iota[None, :, None])
    return (matches.astype(jnp.float32), select)


def per_device(grad_out, top_logits, expert_ids, saved_hidden, w_down):
    count_experts = lax.axis_size("exp")
    slot_count = saved_hidden.shape[2]
    capacity = slot_count // count_experts
    model_width = grad_out.shape[1]
    onehot, select = routing_tables(expert_ids, count_experts, capacity)
    select_wide = select.astype(jnp.float32)
    gate_probs = jax.nn.softmax(top_logits, axis=-1)
    gate_sent = gate_probs.astype(jnp.bfloat16)
    gate_by_expert = jnp.sum(onehot * gate_sent.astype(jnp.float32)[:, :, None], axis=1)
    send_rows = jnp.einsum(
        "ect,td->ecd", select.astype(jnp.bfloat16), grad_out, preferred_element_type=jnp.float32
    ).astype(jnp.bfloat16)
    send_gate = jnp.sum(select_wide * gate_by_expert.T[:, None, :], axis=2).astype(jnp.bfloat16)
    hidden = saved_hidden[0, 0]
    rows_in, gate_in = (
        lax.all_to_all(send_rows, "exp", split_axis=0, concat_axis=0, tiled=True),
        lax.all_to_all(send_gate, "exp", split_axis=0, concat_axis=0, tiled=True),
    )
    flat_rows = rows_in.reshape(slot_count, model_width)
    backprop = lax.dot_general(
        flat_rows,
        lax.all_gather(w_down[0], "ctx", axis=0, tiled=True),
        (((1,), (1,)), ((), ())),
        preferred_element_type=jnp.float32,
    )
    flat_gate = gate_in.reshape(slot_count, 1).astype(jnp.float32)
    hidden_grad = (flat_gate * backprop).astype(jnp.bfloat16)
    slot_grad = jnp.sum(hidden.astype(jnp.float32) * backprop, axis=1)
    scaled = (flat_gate * flat_rows.astype(jnp.float32)).astype(jnp.bfloat16)
    partial_grad = lax.dot_general(
        hidden, scaled, (((0,), (0,)), ((), ())), preferred_element_type=jnp.float32
    )
    weight_grad = lax.psum_scatter(partial_grad, "ctx", scatter_dimension=0, tiled=True)
    returned = lax.all_to_all(
        slot_grad.reshape(count_experts, capacity), "exp", split_axis=0, concat_axis=0, tiled=True
    )
    grad_by_expert = jnp.sum(select_wide * returned[:, :, None], axis=1)
    gate_grad = jnp.sum(onehot * grad_by_expert.T[:, None, :], axis=2)
    logit_grad = gate_probs * (gate_grad - jnp.sum(gate_probs * gate_grad, axis=1, keepdims=True))
    return (logit_grad, hidden_grad.reshape(1, 1, slot_count, -1), weight_grad[None])


def solution(mesh):
    return jax.shard_map(
        per_device,
        mesh=mesh,
        in_specs=(
            P(("ctx", "exp"), None),
            P(("ctx", "exp"), None),
            P(("ctx", "exp"), None),
            P("ctx", "exp", None, None),
            P("exp", "ctx", None),
        ),
        out_specs=(P(("ctx", "exp"), None), P("ctx", "exp", None, None), P("exp", "ctx", None)),
        check_vma=False,
    )
```

profile of v0, /device:TPU:8, one launch (start us, length us, event | category | flops | bytes accessed | tf_op | source)
XLA Modules:
  0.0 434.2 jit_solution(5677177740942893195)
XLA Ops:
  7.2 0.0 copy-start
  7.2 0.0 all-gather.3.cloned.1.call-start
  7.2 0.7 all-gather.3.cloned.1.call-update
  7.9 0.7 convert_reduce_fusion
  8.6 0.1 copy.26
  8.7 0.2 reduce_window_sum.11
  8.9 0.0 copy-done
  9.0 3.4 convolution_convert_fusion
  12.4 0.0 copy-start.2
  12.4 0.0 copy-start.4
  12.4 6.8 %all-to-all-start = ((bf16[8,96,2880]{2,1,0:T(8,128)(2,1)}), bf16[8,96,2880]{2,1,0:T(8,128)(2,1)}, u32[]{:S(2)}, u32[]{:S(2)}) async-start(bf16[8,96,2880]{2,1,0:T(8,128)(2,1)} %convolution_convert_fusion), calls=%async_computation | async-start | bytes 9043968 | tf_op jit(solution)/shard_map/all_to_all | solution.py:33
  19.2 0.0 copy-done.2
  19.2 51.8 %all-to-all-done = bf16[8,96,2880]{2,1,0:T(8,128)(2,1)} async-done(((bf16[8,96,2880]{2,1,0:T(8,128)(2,1)}), bf16[8,96,2880]{2,1,0:T(8,128)(2,1)}, u32[]{:S(2)}, u32[]{:S(2)}) %all-to-all-start) | async-done | bytes 4423712 | tf_op jit(solution)/shard_map/all_to_all | solution.py:33
  71.0 43.6 %all-gather.3.cloned.1.call-done = bf16[1,1536,2880]{2,1,0:T(8,128)(2,1)} async-done(((bf16[1,48,2880]{2,1,0:T(8,128)(2,1)}), bf16[1,1536,2880]{2,1,0:T(8,128)(2,1)}) %all-gather.3.cloned.1.call-update) | async-done | bytes 8847376 | tf_op jit(solution)/shard_map/all_gather | solution.py:39
  114.7 0.0 copy-done.4
  114.7 0.0 copy-start.3
  114.7 13.1 %multiply_reduce_fusion = (f32[768]{0:T(1024)S(1)}, f32[768,1536]{1,0:T(8,128)}) fusion(bf16[1,1,768,1536]{3,2,1,0:T(8,128)(2,1)S(1)} %copy-done.4, bf16[768,2880]{1,0:T(8,128)(2,1)} %bitcast.4, bf16[1,1536,2880]{2,1,0:T(8,128)(2,1)} %all-gather.3.cloned.1.call-done), kind=kOutput, calls=%fused_computation.6 | convolution fusion | flops 6798310400 | bytes 20352000 | tf_op jit(solution)/shard_map/dot_general | solution.py:37
  127.8 0.7 all_to_all.14
  128.4 4.8 %all-to-all-start.1 = ((f32[8,1,96]{2,1,0:T(1,128)}), f32[8,1,96]{2,1,0:T(1,128)S(1)}, u32[]{:S(2)}, u32[]{:S(2)}) async-start(f32[8,1,96]{2,1,0:T(1,128)} %all_to_all.14), calls=%async_computation.1 | async-start | bytes 8192 | tf_op jit(solution)/shard_map/all_to_all | solution.py:51
  133.3 0.0 reduce-scatter.4.cloned.1.call-start
  133.3 0.0 copy-done.3
  133.3 3.7 all-to-all-done.1
  137.0 0.4 select_reduce_fusion
  137.4 7.7 %all_to_all.20 = bf16[8,1,96]{2,1,0:T(2,128)(2,1)S(1)} all-to-all(bf16[8,1,96]{2,1,0:T(2,128)(2,1)S(1)} %copy.29), channel_id=1, replica_groups=mesh['ctx'=32,'exp'=8] {'exp'}, dimensions={0} | all-to-all | bytes 3072 | tf_op jit(solution)/shard_map/all_to_all | solution.py:34
  145.1 3.7 multiply_convert_fusion
  148.8 10.4 %convolution_bitcast_fusion = f32[1536,2880]{0,1:T(8,128)} fusion(bf16[768,2880]{1,0:T(8,128)(2,1)S(1)} %bitcast.34, bf16[1,1,768,1536]{3,2,1,0:T(8,128)(2,1)S(1)} %copy-done.4), kind=kOutput, calls=%fused_computation | convolution fusion | flops 6794772480 | bytes 24477696 | tf_op jit(solution)/shard_map/dot_general | solution.py:47
  159.1 18.1 %copy.31 = f32[1536,2880]{1,0:T(8,128)} copy(f32[1536,2880]{0,1:T(8,128)} %convolution_bitcast_fusion) | data formatting | bytes 35389440
  177.2 0.0 reduce-scatter.4.cloned.1.call-update
  177.3 0.6 subtract_multiply_fusion
  177.9 0.1 reshape.60
  178.0 0.0 copy-start.1
  178.0 4.1 fusion.2
  182.1 242.5 %reduce-scatter.4.cloned.1.call-done = f32[48,2880]{1,0:T(8,128)} async-done(((f32[1536,2880]{1,0:T(8,128)}), f32[48,2880]{1,0:T(8,128)}) %reduce-scatter.4.cloned.1.call-update) | async-done | bytes 552976
  424.6 1.5 copy.32
  426.1 1.3 copy.30
  427.4 0.0 copy-done.1
  (12 shorter events, 0.2 us)
Async XLA Ops:
  7.2 1.8 copy-start
  7.2 107.5 %all-gather.3.cloned.1.call-start = ((), (), s32[]{:S(2)}) async-start(), calls=%async_computation.4 | async-start | bytes 9326592 | tf_op jit(solution)/shard_map/all_gather | solution.py:39
  12.4 6.8 %copy-start.2 = (f32[128,4]{0,1:T(4,128)S(1)}, f32[128,4]{0,1:T(4,128)}, u32[]{:S(2)}) copy-start(f32[128,4]{0,1:T(4,128)} %param.6) | copy-start | bytes 6148
  12.4 102.3 %copy-start.4 = (bf16[1,1,768,1536]{3,2,1,0:T(8,128)(2,1)S(1)}, bf16[1,1,768,1536]{3,2,1,0:T(8,128)(2,1)}, u32[]{:S(2)}) copy-start(bf16[1,1,768,1536]{3,2,1,0:T(8,128)(2,1)} %param.8) | copy-start | bytes 7077892
  12.4 58.6 %all-to-all-start = ((bf16[8,96,2880]{2,1,0:T(8,128)(2,1)}), bf16[8,96,2880]{2,1,0:T(8,128)(2,1)}, u32[]{:S(2)}, u32[]{:S(2)}) async-start(bf16[8,96,2880]{2,1,0:T(8,128)(2,1)} %convolution_convert_fusion), calls=%async_computation | async-start | bytes 9043968 | tf_op jit(solution)/shard_map/all_to_all | solution.py:33
  114.7 18.6 %copy-start.3 = (s32[128,4]{0,1:T(4,128)S(1)}, s32[128,4]{0,1:T(4,128)}, u32[]{:S(2)}) copy-start(s32[128,4]{0,1:T(4,128)} %param.7) | copy-start | bytes 6148
  128.4 8.6 %all-to-all-start.1 = ((f32[8,1,96]{2,1,0:T(1,128)}), f32[8,1,96]{2,1,0:T(1,128)S(1)}, u32[]{:S(2)}, u32[]{:S(2)}) async-start(f32[8,1,96]{2,1,0:T(1,128)} %all_to_all.14), calls=%async_computation.1 | async-start | bytes 8192 | tf_op jit(solution)/shard_map/all_to_all | solution.py:51
  133.3 291.3 %reduce-scatter.4.cloned.1.call-start = ((), (), s32[]{:S(2)}) async-start(), calls=%async_computation.5 | async-start | bytes 18653184
  178.0 249.4 %copy-start.1 = (bf16[128,2880]{0,1:T(8,128)(2,1)S(1)}, bf16[128,2880]{0,1:T(8,128)(2,1)}, u32[]{:S(2)}) copy-start(bf16[128,2880]{0,1:T(8,128)(2,1)} %param.5) | copy-start | bytes 2211844
Sparse Core Ops, SparseCore 0:
  10.6 104.0 all-gather.2
  177.4 247.1 reduce-scatter.3
where the time goes:
time: 435 us; the launch traced here: 434 us
  waiting for transfers between devices  342 us (79%)
  matrix products  26.9 us (6%)
  local copies, waits for them, and re-layouts  21.8 us (5%)
  between operations  14.1 us (3%)
  starting transfers between devices  11.7 us (3%)
  other arithmetic  9.78 us (2%)
  blocking collectives  7.66 us (2%)
    unnamed x3, waiting for transfers between devices  243 us
    all_to_all x1, waiting for transfers between devices, per_device(): lax.all_to_all(send_rows, 'exp', split_axis=0, concat_axis=0, tiled=True)  51.8 us
    all_gather x1, waiting for transfers between devices, per_device(): lax.all_gather(w_down[0], 'ctx', axis=0, tiled=True)  43.6 us
    unnamed x13, local copies, waits for them, and re-layouts  20.9 us
    dot_general x1, matrix products, per_device(): lax.dot_general(flat_rows, lax.all_gather(w_down[0], 'ctx', axis=0, tiled...  13.1 us
    dot_general x1, matrix products, per_device(): lax.dot_general(hidden, scaled, (((0,), (0,)), ((), ())), preferred_eleme...  10.4 us
  transfers between devices with their start and end apart: 4, of which 4 were waited for; matrix products, arithmetic and copies ran while one was open for 2% of the time, Pallas kernels for 0%

commit v1 on v0

--- a/solution.py
+++ b/solution.py
@@ -36,7 +36,9 @@
     flat_rows = rows_in.reshape(slot_count, model_width)
     backprop = lax.dot_general(
         flat_rows,
-        lax.all_gather(w_down[0], "ctx", axis=0, tiled=True),
+        jnp.concatenate(
+            lax.all_to_all(jnp.stack([w_down[0]] * lax.axis_size("ctx")), "ctx", 0, 0), axis=0
+        ),
         (((1,), (1,)), ((), ())),
         preferred_element_type=jnp.float32,
     )

time: 435 us -> 618 us (1.42)
  waiting for transfers between devices: 342 us -> 462 us
  blocking collectives: 7.66 us -> 65.6 us
    all_to_all x1, waiting for transfers between devices: 51.8 us -> 203 us  [per_device(): lax.all_to_all(jnp.stack([w_down[0]] * lax.axis_size('ctx')), 'ctx', 0, 0)]
    all_to_all x0 -> x1, blocking collectives: none -> 57.9 us  [per_device(): lax.all_to_all(send_rows, 'exp', split_axis=0, concat_axis=0, tiled=True)]
    all_gather x1 -> x0, waiting for transfers between devices: 43.6 us -> none  [per_device(): lax.all_gather(w_down[0], 'ctx', axis=0, tiled=True)]
    unnamed x3 -> x2, waiting for transfers between devices: 243 us -> 256 us
    unnamed x13 -> x15, local copies, waits for them, and re-layouts: 20.9 us -> 20.9 us
  transfers between devices with their start and end apart: 4 -> 3, of which waited for: 4 -> 3; matrix products, arithmetic and copies ran while one was open for 2% -> 1% of each run, Pallas kernels for 0% -> 0%
where the time goes in v1:
time: 618 us
  waiting for transfers between devices  462 us (75%)
  blocking collectives  65.6 us (11%)
  local copies, waits for them, and re-layouts  25.9 us (4%)
  matrix products  24.8 us (4%)
  starting transfers between devices  15 us (2%)
  between operations  14.1 us (2%)
  other arithmetic  9.86 us (2%)
    unnamed x2, waiting for transfers between devices  256 us
    all_to_all x1, waiting for transfers between devices, per_device(): lax.all_to_all(jnp.stack([w_down[0]] * lax.axis_size('ctx')), 'ctx', 0, 0)  203 us
    all_to_all x1, blocking collectives, per_device(): lax.all_to_all(send_rows, 'exp', split_axis=0, concat_axis=0, tiled=True)  57.9 us
    unnamed x15, local copies, waits for them, and re-layouts  20.9 us
    dot_general x1, matrix products, per_device(): lax.dot_general(flat_rows, jnp.concatenate(lax.all_to_all(jnp.stack([w_do...  13.1 us
  transfers between devices with their start and end apart: 3, of which 3 were waited for; matrix products, arithmetic and copies ran while one was open for 1% of the time, Pallas kernels for 0%

profile of v1, /device:TPU:8, one launch (start us, length us, event | category | flops | bytes accessed | tf_op | source)
XLA Modules:
  0.0 617.6 jit_solution(8847469725952639819)
XLA Ops:
  7.2 0.0 copy-start
  7.2 0.8 convert_reduce_fusion
  8.0 0.1 copy.26
  8.1 0.2 reduce_window_sum.11
  8.3 0.0 copy-done
  8.3 1.3 convolution_convert_fusion
  9.7 0.0 copy-start.2
  9.7 57.9 %all_to_all.25 = bf16[8,96,2880]{2,1,0:T(8,128)(2,1)} all-to-all(bf16[8,96,2880]{2,1,0:T(8,128)(2,1)S(1)} %convolution_convert_fusion), channel_id=1, replica_groups=mesh['ctx'=32,'exp'=8] {'exp'}, dimensions={0} | all-to-all | bytes 8847360 | tf_op jit(solution)/shard_map/all_to_all | solution.py:33
  67.6 0.0 copy-done.2
  67.6 4.1 stack.3
  71.7 0.0 copy-start.3
  71.7 0.0 copy-start.5
  71.7 10.9 %all-to-all-start.1 = ((bf16[32,48,2880]{2,1,0:T(8,128)(2,1)}), bf16[32,48,2880]{2,1,0:T(8,128)(2,1)}, u32[]{:S(2)}, u32[]{:S(2)}) async-start(bf16[32,48,2880]{2,1,0:T(8,128)(2,1)} %stack.3), calls=%async_computation.1 | async-start | bytes 18087936 | tf_op jit(solution)/shard_map/all_to_all | solution.py:40
  82.6 0.0 copy-done.3
  82.7 202.9 %all-to-all-done.1 = bf16[32,48,2880]{2,1,0:T(8,128)(2,1)} async-done(((bf16[32,48,2880]{2,1,0:T(8,128)(2,1)}), bf16[32,48,2880]{2,1,0:T(8,128)(2,1)}, u32[]{:S(2)}, u32[]{:S(2)}) %all-to-all-start.1) | async-done | bytes 8847392 | tf_op jit(solution)/shard_map/all_to_all | solution.py:40
  285.6 0.0 copy-done.5
  285.6 0.0 copy-start.4
  285.6 13.1 %multiply_reduce_fusion = (f32[768]{0:T(1024)S(1)}, f32[768,1536]{1,0:T(8,128)}) fusion(bf16[1,1,768,1536]{3,2,1,0:T(8,128)(2,1)S(1)} %copy-done.5, bf16[768,2880]{1,0:T(8,128)(2,1)} %bitcast.31, bf16[1536,2880]{1,0:T(8,128)(2,1)} %bitcast.6), kind=kOutput, calls=%fused_computation.4 | convolution fusion | flops 6798310400 | bytes 20352000 | tf_op jit(solution)/shard_map/dot_general | solution.py:37
  298.7 0.7 all_to_all.18
  299.3 4.1 all-to-all-start.2
  303.4 0.0 reduce-scatter.4.cloned.1.call-start
  303.4 0.0 copy-done.4
  303.5 3.8 all-to-all-done.2
  307.2 0.4 select_reduce_fusion
  307.6 7.6 %all_to_all.26 = bf16[8,1,96]{2,1,0:T(2,128)(2,1)S(1)} all-to-all(bf16[8,1,96]{2,1,0:T(2,128)(2,1)S(1)} %copy.29), channel_id=1, replica_groups=mesh['ctx'=32,'exp'=8] {'exp'}, dimensions={0} | all-to-all | bytes 3072 | tf_op jit(solution)/shard_map/all_to_all | solution.py:34
  315.2 3.7 multiply_convert_fusion
  318.9 10.4 %convolution_bitcast_fusion = f32[1536,2880]{0,1:T(8,128)} fusion(bf16[768,2880]{1,0:T(8,128)(2,1)S(1)} %bitcast.33, bf16[1,1,768,1536]{3,2,1,0:T(8,128)(2,1)S(1)} %copy-done.5), kind=kOutput, calls=%fused_computation | convolution fusion | flops 6794772480 | bytes 24477696 | tf_op jit(solution)/shard_map/dot_general | solution.py:49
  329.3 18.1 %copy.31 = f32[1536,2880]{1,0:T(8,128)} copy(f32[1536,2880]{0,1:T(8,128)} %convolution_bitcast_fusion) | data formatting | bytes 35389440
  347.4 0.0 reduce-scatter.4.cloned.1.call-update
  347.5 0.6 subtract_multiply_fusion
  348.1 0.1 reshape.65
  348.2 0.0 copy-start.1
  348.2 4.1 fusion
  352.3 255.7 %reduce-scatter.4.cloned.1.call-done = f32[48,2880]{1,0:T(8,128)} async-done(((f32[1536,2880]{1,0:T(8,128)}), f32[48,2880]{1,0:T(8,128)}) %reduce-scatter.4.cloned.1.call-update) | async-done | bytes 552976
  608.0 1.5 copy.32
  609.5 1.3 copy.30
  610.8 0.0 copy-done.1
  (12 shorter events, 0.2 us)
Async XLA Ops:
  7.2 1.1 copy-start
  9.7 57.9 %copy-start.2 = (bf16[1,48,2880]{2,1,0:T(8,128)(2,1)S(1)}, bf16[1,48,2880]{2,1,0:T(8,128)(2,1)}, u32[]{:S(2)}) copy-start(bf16[1,48,2880]{2,1,0:T(8,128)(2,1)} %param.9) | copy-start | bytes 829444
  71.7 10.9 %copy-start.3 = (f32[128,4]{0,1:T(4,128)S(1)}, f32[128,4]{0,1:T(4,128)}, u32[]{:S(2)}) copy-start(f32[128,4]{0,1:T(4,128)} %param.6) | copy-start | bytes 6148
  71.7 213.9 %copy-start.5 = (bf16[1,1,768,1536]{3,2,1,0:T(8,128)(2,1)S(1)}, bf16[1,1,768,1536]{3,2,1,0:T(8,128)(2,1)}, u32[]{:S(2)}) copy-start(bf16[1,1,768,1536]{3,2,1,0:T(8,128)(2,1)} %param.8) | copy-start | bytes 7077892
  71.7 213.9 %all-to-all-start.1 = ((bf16[32,48,2880]{2,1,0:T(8,128)(2,1)}), bf16[32,48,2880]{2,1,0:T(8,128)(2,1)}, u32[]{:S(2)}, u32[]{:S(2)}) async-start(bf16[32,48,2880]{2,1,0:T(8,128)(2,1)} %stack.3), calls=%async_computation.1 | async-start | bytes 18087936 | tf_op jit(solution)/shard_map/all_to_all | solution.py:40
  285.6 17.9 %copy-start.4 = (s32[128,4]{0,1:T(4,128)S(1)}, s32[128,4]{0,1:T(4,128)}, u32[]{:S(2)}) copy-start(s32[128,4]{0,1:T(4,128)} %param.7) | copy-start | bytes 6148
  299.3 7.9 %all-to-all-start.2 = ((f32[8,1,96]{2,1,0:T(1,128)}), f32[8,1,96]{2,1,0:T(1,128)S(1)}, u32[]{:S(2)}, u32[]{:S(2)}) async-start(f32[8,1,96]{2,1,0:T(1,128)} %all_to_all.18), calls=%async_computation.2 | async-start | bytes 8192 | tf_op jit(solution)/shard_map/all_to_all | solution.py:53
  303.4 304.6 %reduce-scatter.4.cloned.1.call-start = ((), (), s32[]{:S(2)}) async-start(), calls=%async_computation.5 | async-start | bytes 18653184
  348.2 262.6 %copy-start.1 = (bf16[128,2880]{0,1:T(8,128)(2,1)S(1)}, bf16[128,2880]{0,1:T(8,128)(2,1)}, u32[]{:S(2)}) copy-start(bf16[128,2880]{0,1:T(8,128)(2,1)} %param.5) | copy-start | bytes 2211844
Sparse Core Ops, SparseCore 0:
  347.6 260.3 reduce-scatter.3
